TPU v7x, 32 devices: a whole 2x2x4 slice. The times are simulated.
32 devices in a mesh: row: 4 (over z), col: 8 (over y, x, core).
Axes of the slice: x: 2, y: 2, z: 4, core: 2. Of those that a mesh axis runs over, the one named last changes fastest.
Arguments:
- slip_load: bfloat16 [4, 8, 1024, 128], P('row', 'col'), may hold values from -6 to 6
- flexibility: bfloat16 [4, 8, 1024, 1024], P('row', 'col'), as said below
- schur: bfloat16 [4, 8, 1024, 1024], P('row', 'col'), as said below
- corner_coupling: float32 [4, 8, 12, 1024], P('row', 'col'), may hold values from -0.1875 to 0.1875
- coarse_inverse: float32 [384, 384], P('row', 'col'), as said below
- bounds_table: float32 [16], replicated, may hold values from 0.3 to 3
- bound_index: int32 [4, 8, 1024], P('row', 'col'), may hold values from 0 to 15
- face_rows: int32 [4, 8, 4], P('row', 'col'), may hold values from 0 to 256, as said below
Outputs:
- multipliers: bfloat16 [4, 8, 1024, 128], P('row', 'col')
Inputs may be any that keep to these rules, and one draw needn't show every extreme that they name: `face_rows`: face counts agree between the two subdomains of a shared face, are 0 on faces at the edge of the grid, and some face has exactly 256 live slots. `coarse_inverse`: symmetric. `flexibility`: symmetric and positive definite. `schur`: symmetric and positive definite.
All inputs are finite; a program needn't handle non-finite values.
Results may differ from a plain program's by a relative error of at most 0.0038.
Values sent between devices are 32-bit elements; how exact they have to be, the bound alone decides.
No kernel may reach another device: no remote copies, remote signals or barrier semaphores. Data moves between devices by JAX's collectives and lax.ppermute only.
A program may use at most 64 MiB of HBM per device.

v0:
```python
import jax
import jax.numpy as jnp
from jax import lax
from jax.sharding import PartitionSpec as P

ITERS = 2


def passed_along(x, axis, by):
    count = lax.axis_size(axis)
    pairs = [(i, i + by) for i in range(count) if 0 <= i + by < count]
    return lax.ppermute(x, axis, pairs)


def broadcast(block, axis, holder):
    block = jnp.where(lax.axis_index(axis) == holder, block, jnp.zeros_like(block))
    return lax.psum(block, axis)


def local(
    slip_load,
    flexibility,
    schur,
    corner_coupling,
    coarse_inverse,
    bounds_table,
    bound_index,
    face_rows,
):
    loads = slip_load[0, 0].astype(jnp.float32)
    flex_block = flexibility[0, 0]
    schur_block = schur[0, 0]
    coupling = corner_coupling[0, 0]
    row_count = flex_block.shape[0]
    face_size = row_count // 4
    corners = coupling.shape[0]
    row_devices = lax.axis_size("row")
    row_index = lax.axis_index("row")
    col_index = lax.axis_index("col")
    levels = jnp.arange(bounds_table.shape[0], dtype=jnp.int32)
    onehot = (bound_index[0, 0][:, None] == levels[None, :]).astype(jnp.float32)
    bound = jnp.sum(onehot * bounds_table[None, :], axis=1)[:, None]
    slots = jnp.arange(face_size, dtype=jnp.int32)
    live = (slots[None, :] < face_rows[0, 0][:, None]).astype(jnp.float32).reshape(row_count, 1)
    lam = jnp.clip(loads, -bound, bound)
    for iteration in range(ITERS):
        displacement = jnp.dot(
            flex_block, lam.astype(jnp.bfloat16), preferred_element_type=jnp.float32
        )
        nb_west = passed_along(displacement[face_size : 2 * face_size], "col", 1)
        nb_east = passed_along(displacement[0:face_size], "col", -1)
        nb_lower = passed_along(displacement[3 * face_size :], "row", 1)
        nb_upper = passed_along(displacement[2 * face_size : 3 * face_size], "row", -1)
        paired = jnp.concatenate([nb_west, nb_east, nb_lower, nb_upper], axis=0)
        jump = live * (displacement - paired - loads)
        corner_force = jnp.dot(coupling, jump, precision=lax.Precision.HIGHEST)
        gathered = lax.all_gather(corner_force, "row", axis=0, tiled=True)
        partial_value = jnp.dot(coarse_inverse, gathered, precision=lax.Precision.HIGHEST)
        total = lax.psum(partial_value, "col")
        picked = broadcast(total, "row", col_index // 2)
        offset = col_index % 2 * (corners * row_devices) + row_index * corners
        coarse = lax.dynamic_slice_in_dim(picked, offset, corners, 0)
        correction = lax.dot_general(
            coupling, coarse, (((0,), (0,)), ((), ())), precision=lax.Precision.HIGHEST
        )
        projected = jump - correction
        projected_b = projected.astype(jnp.bfloat16)
        search = jnp.dot(schur_block, projected_b, preferred_element_type=jnp.float32)
        gain_local = jnp.sum(projected_b.astype(jnp.float32) * search, axis=0)
        search_b = search.astype(jnp.bfloat16)
        gain = lax.psum(gain_local, ("row", "col"))
        curved = jnp.dot(flex_block, search_b, preferred_element_type=jnp.float32)
        curvature = lax.psum(jnp.sum(search_b.astype(jnp.float32) * curved, axis=0), ("row", "col"))
        lam = jnp.clip(lam - (gain / curvature)[None, :] * search, -bound, bound)
    return lam.astype(jnp.bfloat16)[None, None]


def solution(mesh):
    return jax.shard_map(
        local,
        mesh=mesh,
        in_specs=(
            P("row", "col", None, None),
            P("row", "col", None, None),
            P("row", "col", None, None),
            P("row", "col", None, None),
            P("row", "col"),
            P(),
            P("row", "col", None),
            P("row", "col", None),
        ),
        out_specs=P("row", "col", None, None),
        check_vma=False,
    )
```

profile of v0, /device:TPU:14, one launch (start us, length us, event | category | flops | bytes accessed | tf_op | source)
XLA Modules:
  0.0 235.4 jit_solution(16768184671712670383)
XLA Ops:
  0.0 0.9 select_reduce_fusion
  1.0 1.1 copy.15
  2.1 2.4 %fusion.14 = f32[1024,128]{0,1:T(8,128)S(1)} fusion(bf16[1,1,1024,1024]{3,2,1,0:T(8,128)(2,1)} %param.9, bf16[1,1,1024,128]{2,3,1,0:T(8,128)(2,1)S(1)} %copy.15, f32[1024]{0:T(1024)S(1)} %neg.10, f32[1024]{0:T(1024)S(1)} %select_reduce_fusion), kind=kOutput, calls=%fused_computation.16 | convolution fusion | flops 269221888 | bytes 2891776 | tf_op jit(solution)/shard_map/dot_general | solution.py:47
  5.3 1.9 collective-permute-start
  7.2 2.4 %collective-permute-start.3 = (f32[256,128]{0,1:T(8,128)}, f32[256,128]{0,1:T(8,128)S(1)}, u32[]{:S(2)}, u32[]{:S(2)}) collective-permute-start(f32[256,128]{0,1:T(8,128)} %get-tuple-element.14), channel_id=1, source_target_pairs={{8,0},{16,8},{24,16},{9,1},{17,9},{25,17},{10,2},{18,10},{26,18},{... | collective-permute-start | bytes 393224 | tf_op jit(solution)/shard_map/ppermute | solution.py:12
  9.6 3.5 %collective-permute-start.2 = (f32[256,128]{0,1:T(8,128)}, f32[256,128]{0,1:T(8,128)S(1)}, u32[]{:S(2)}, u32[]{:S(2)}) collective-permute-start(f32[256,128]{0,1:T(8,128)} %get-tuple-element.15), channel_id=1, source_target_pairs={{0,8},{8,16},{16,24},{1,9},{9,17},{17,25},{2,10},{10,18},{18,26},{... | collective-permute-start | bytes 393224 | tf_op jit(solution)/shard_map/ppermute | solution.py:12
  13.1 3.1 %collective-permute-start.1 = (f32[256,128]{0,1:T(8,128)S(1)}, f32[256,128]{0,1:T(8,128)}, u32[]{:S(2)}, u32[]{:S(2)}) collective-permute-start(f32[256,128]{0,1:T(8,128)S(1)} %get-tuple-element.16), channel_id=1, source_target_pairs={{1,0},{2,1},{3,2},{4,3},{5,4},{6,5},{7,6},{9,8},{10,9},{11,10},{12... | collective-permute-start | bytes 393224 | tf_op jit(solution)/shard_map/ppermute | solution.py:12
  16.6 2.0 collective-permute-done.1
  18.7 1.5 convolution_bitcast_fusion.5
  20.1 11.5 %all-gather = f32[4,12,128]{2,1,0:T(8,128)S(1)} all-gather(f32[1,12,128]{2,1,0:T(8,128)S(1)} %convolution_bitcast_fusion.5), channel_id=1, replica_groups=mesh['row'=4,'col'=8] {'row'}, dimensions={0}, use_global_device_ids=true | all-gather | bytes 30720 | tf_op jit(solution)/shard_map/all_gather | solution.py:57
  31.9 21.2 %psum.56 = f32[96,128]{1,0:T(8,128)S(1)} all-reduce(f32[96,128]{1,0:T(8,128)S(1)} %convolution_bitcast_fusion.3), channel_id=1, replica_groups=mesh['row'=4,'col'=8] {'col'}, use_global_device_ids=true, to_apply=%region_1.2 | all-reduce | flops 12288 | bytes 98304 | tf_op jit(solution)/shard_map/psum | solution.py:59
  53.1 16.4 %psum.57 = f32[96,128]{1,0:T(8,128)S(1)} all-reduce(f32[96,128]{1,0:T(8,128)S(1)} %broadcast_select_fusion.1), channel_id=1, replica_groups=mesh['row'=4,'col'=8] {'row'}, use_global_device_ids=true, to_apply=%region_2.3 | all-reduce | flops 12288 | bytes 98304 | tf_op jit(solution)/shard_map/psum | solution.py:17
  69.5 1.7 fusion.39
  71.2 0.9 multiply_reduce_fusion.1
  72.1 0.9 fusion.40
  73.0 44.6 %all-reduce.1 = (f32[128]{0:T(128)S(1)}, f32[128]{0:T(128)S(1)}) all-reduce(f32[128]{0:T(128)S(1)} %get-tuple-element.17, f32[128]{0:T(128)S(1)} %fusion.40), channel_id=1, replica_groups=mesh['row'=4,'col'=8] {'row','col'}, use_global_device_ids=true, to_apply=%region_4.5 | all-reduce | flops 256 | bytes 2048 | tf_op jit(solution)/shard_map/psum | solution.py:71
  117.7 2.4 %fusion.20 = f32[1024,128]{0,1:T(8,128)S(1)} fusion(bf16[1,1,1024,1024]{3,2,1,0:T(8,128)(2,1)} %param.9, bf16[1,1,1024,128]{2,3,1,0:T(8,128)(2,1)S(1)} %copy.15, f32[1024,128]{0,1:T(8,128)S(1)} %get-tuple-element.18, f32[128]{0:T(128)S(1)} %div.18, f32[1024]{0:T(1024)S(1)} %neg.10, f32[1024]{0:T(1024)S(1)} %select_reduce_fusion), kind=kOutput, calls=%fused_computation.18 | convolution fusion | flops 269484032 | bytes 3416576 | tf_op jit(solution)/shard_map/dot_general | solution.py:47
  120.2 1.9 collective-permute-start.4
  122.1 1.9 collective-permute-start.7
  124.0 3.9 %collective-permute-start.6 = (f32[256,128]{0,1:T(8,128)S(1)}, f32[256,128]{0,1:T(8,128)S(1)}, u32[]{:S(2)}, u32[]{:S(2)}) collective-permute-start(f32[256,128]{0,1:T(8,128)S(1)} %get-tuple-element.11), channel_id=1, source_target_pairs={{0,8},{8,16},{16,24},{1,9},{9,17},{17,25},{2,10},{10,18},{18,26},{... | collective-permute-start | bytes 393224 | tf_op jit(solution)/shard_map/ppermute | solution.py:12
  128.0 3.1 %collective-permute-start.5 = (f32[256,128]{0,1:T(8,128)S(1)}, f32[256,128]{0,1:T(8,128)S(1)}, u32[]{:S(2)}, u32[]{:S(2)}) collective-permute-start(f32[256,128]{0,1:T(8,128)S(1)} %get-tuple-element.12), channel_id=1, source_target_pairs={{1,0},{2,1},{3,2},{4,3},{5,4},{6,5},{7,6},{9,8},{10,9},{11,10},{12... | collective-permute-start | bytes 393224 | tf_op jit(solution)/shard_map/ppermute | solution.py:12
  131.1 2.4 %collective-permute-done.5 = f32[256,128]{0,1:T(8,128)S(1)} collective-permute-done((f32[256,128]{0,1:T(8,128)S(1)}, f32[256,128]{0,1:T(8,128)S(1)}, u32[]{:S(2)}, u32[]{:S(2)}) %collective-permute-start.5) | collective-permute-done | bytes 131104 | tf_op jit(solution)/shard_map/ppermute | solution.py:12
  134.2 11.3 %all-gather.1 = f32[4,12,128]{2,1,0:T(8,128)S(1)} all-gather(f32[1,12,128]{2,1,0:T(8,128)S(1)} %convolution_bitcast_fusion.4), channel_id=1, replica_groups=mesh['row'=4,'col'=8] {'row'}, dimensions={0}, use_global_device_ids=true | all-gather | bytes 30720 | tf_op jit(solution)/shard_map/all_gather | solution.py:57
  146.1 1.0 convolution_bitcast_fusion.2
  147.2 20.5 %psum.60 = f32[96,128]{1,0:T(8,128)S(1)} all-reduce(f32[96,128]{1,0:T(8,128)S(1)} %convolution_bitcast_fusion.2), channel_id=1, replica_groups=mesh['row'=4,'col'=8] {'col'}, use_global_device_ids=true, to_apply=%region_7.8 | all-reduce | flops 12288 | bytes 98304 | tf_op jit(solution)/shard_map/psum | solution.py:59
  167.7 16.3 %psum.61 = f32[96,128]{1,0:T(8,128)S(1)} all-reduce(f32[96,128]{1,0:T(8,128)S(1)} %broadcast_select_fusion), channel_id=1, replica_groups=mesh['row'=4,'col'=8] {'row'}, use_global_device_ids=true, to_apply=%region_8.9 | all-reduce | flops 12288 | bytes 98304 | tf_op jit(solution)/shard_map/psum | solution.py:17
  184.0 1.9 fusion.38
  185.9 0.9 multiply_reduce_fusion
  186.9 0.9 fusion.43
  187.8 44.8 %all-reduce = (f32[128]{0:T(128)S(1)}, f32[128]{0:T(128)S(1)}) all-reduce(f32[128]{0:T(128)S(1)} %get-tuple-element.19, f32[128]{0:T(128)S(1)} %fusion.43), channel_id=1, replica_groups=mesh['row'=4,'col'=8] {'row','col'}, use_global_device_ids=true, to_apply=%region_10.11 | all-reduce | flops 256 | bytes 2048 | tf_op jit(solution)/shard_map/psum | solution.py:71
  232.6 1.0 fusion.57
  233.6 1.8 copy.16
  (53 shorter events, 2.8 us)
Async XLA Ops:
  0.0 71.2 %copy-start = (bf16[1,1,1024,1024]{3,2,1,0:T(8,128)(2,1)S(1)}, bf16[1,1,1024,1024]{3,2,1,0:T(8,128)(2,1)}, u32[]{:S(2)}) copy-start(bf16[1,1,1024,1024]{3,2,1,0:T(8,128)(2,1)} %param.10) | copy-start | bytes 6291460
  0.9 116.7 %copy-start.8 = (f32[1024]{0:T(1024)}, f32[1024]{0:T(1024)S(1)}, u32[]{:S(2)}) copy-start(f32[1024]{0:T(1024)S(1)} %select_reduce_fusion) | copy-start | bytes 12292
  1.0 116.7 %copy-start.11 = (f32[1024]{0:T(1024)}, f32[1024]{0:T(1024)S(1)}, u32[]{:S(2)}) copy-start(f32[1024]{0:T(1024)S(1)} %neg.10) | copy-start | bytes 12292
  2.1 14.1 %copy-start.16 = (s32[1,1,4]{2,1,0:T(1,128)S(1)}, s32[1,1,4]{2,1,0:T(1,128)}, u32[]{:S(2)}) copy-start(s32[1,1,4]{2,1,0:T(1,128)} %param.15) | copy-start | bytes 52
  2.1 16.6 %copy-start.3 = (f32[1,1,12,1024]{3,1,2,0:T(1,128)S(1)}, f32[1,1,12,1024]{3,1,2,0:T(1,128)}, u32[]{:S(2)}) copy-start(f32[1,1,12,1024]{3,1,2,0:T(1,128)} %param.11) | copy-start | bytes 147460
  2.1 29.5 %copy-start.10 = (f32[96,48]{0,1:T(8,128)S(1)}, f32[96,48]{0,1:T(8,128)}, u32[]{:S(2)}) copy-start(f32[96,48]{0,1:T(8,128)} %param.12) | copy-start | bytes 55300
  5.3 11.0 %collective-permute-start = (f32[256,128]{0,1:T(8,128)}, f32[256,128]{0,1:T(8,128)S(1)}, u32[]{:S(2)}, u32[]{:S(2)}) collective-permute-start(f32[256,128]{0,1:T(8,128)} %get-tuple-element.13), channel_id=1, source_target_pairs={{0,1},{1,2},{2,3},{3,4},{4,5},{5,6},{6,7},{8,9},{9,10},{10,11},{11... | collective-permute-start | bytes 393224 | tf_op jit(solution)/shard_map/ppermute | solution.py:12
  7.2 9.1 %collective-permute-start.3 = (f32[256,128]{0,1:T(8,128)}, f32[256,128]{0,1:T(8,128)S(1)}, u32[]{:S(2)}, u32[]{:S(2)}) collective-permute-start(f32[256,128]{0,1:T(8,128)} %get-tuple-element.14), channel_id=1, source_target_pairs={{8,0},{16,8},{24,16},{9,1},{17,9},{25,17},{10,2},{18,10},{26,18},{... | collective-permute-start | bytes 393224 | tf_op jit(solution)/shard_map/ppermute | solution.py:12
  9.6 7.1 %collective-permute-start.2 = (f32[256,128]{0,1:T(8,128)}, f32[256,128]{0,1:T(8,128)S(1)}, u32[]{:S(2)}, u32[]{:S(2)}) collective-permute-start(f32[256,128]{0,1:T(8,128)} %get-tuple-element.15), channel_id=1, source_target_pairs={{0,8},{8,16},{16,24},{1,9},{9,17},{17,25},{2,10},{10,18},{18,26},{... | collective-permute-start | bytes 393224 | tf_op jit(solution)/shard_map/ppermute | solution.py:12
  13.1 5.6 %collective-permute-start.1 = (f32[256,128]{0,1:T(8,128)S(1)}, f32[256,128]{0,1:T(8,128)}, u32[]{:S(2)}, u32[]{:S(2)}) collective-permute-start(f32[256,128]{0,1:T(8,128)S(1)} %get-tuple-element.16), channel_id=1, source_target_pairs={{1,0},{2,1},{3,2},{4,3},{5,4},{6,5},{7,6},{9,8},{10,9},{11,10},{12... | collective-permute-start | bytes 393224 | tf_op jit(solution)/shard_map/ppermute | solution.py:12
  16.3 117.3 %copy-start.13 = (f32[1,2,4,128]{3,1,2,0:T(2,128)}, f32[1,2,4,128]{3,1,2,0:T(2,128)S(1)}, u32[]{:S(2)}) copy-start(f32[1,2,4,128]{3,1,2,0:T(2,128)S(1)} %copy.18) | copy-start | bytes 12292
  69.5 2.6 %copy-start.1 = (bf16[1,1,1024,1024]{3,2,1,0:T(8,128)(2,1)S(1)}, bf16[1,1,1024,1024]{3,2,1,0:T(8,128)(2,1)}, u32[]{:S(2)}) copy-start(bf16[1,1,1024,1024]{3,2,1,0:T(8,128)(2,1)} %param.9) | copy-start | bytes 6291460
  117.7 2.5 %copy-start.14 = (f32[128]{0:T(128)}, f32[128]{0:T(128)S(1)}, u32[]{:S(2)}) copy-start(f32[128]{0:T(128)S(1)} %div.18) | copy-start | bytes 1540
  120.2 10.9 %collective-permute-start.4 = (f32[256,128]{0,1:T(8,128)S(1)}, f32[256,128]{0,1:T(8,128)S(1)}, u32[]{:S(2)}, u32[]{:S(2)}) collective-permute-start(f32[256,128]{0,1:T(8,128)S(1)} %get-tuple-element.9), channel_id=1, source_target_pairs={{0,1},{1,2},{2,3},{3,4},{4,5},{5,6},{6,7},{8,9},{9,10},{10,11},{11... | collective-permute-start | bytes 393224 | tf_op jit(solution)/shard_map/ppermute | solution.py:12
  122.1 9.0 %collective-permute-start.7 = (f32[256,128]{0,1:T(8,128)S(1)}, f32[256,128]{0,1:T(8,128)S(1)}, u32[]{:S(2)}, u32[]{:S(2)}) collective-permute-start(f32[256,128]{0,1:T(8,128)S(1)} %get-tuple-element.10), channel_id=1, source_target_pairs={{8,0},{16,8},{24,16},{9,1},{17,9},{25,17},{10,2},{18,10},{26,18},{... | collective-permute-start | bytes 393224 | tf_op jit(solution)/shard_map/ppermute | solution.py:12
  124.0 7.1 %collective-permute-start.6 = (f32[256,128]{0,1:T(8,128)S(1)}, f32[256,128]{0,1:T(8,128)S(1)}, u32[]{:S(2)}, u32[]{:S(2)}) collective-permute-start(f32[256,128]{0,1:T(8,128)S(1)} %get-tuple-element.11), channel_id=1, source_target_pairs={{0,8},{8,16},{16,24},{1,9},{9,17},{17,25},{2,10},{10,18},{18,26},{... | collective-permute-start | bytes 393224 | tf_op jit(solution)/shard_map/ppermute | solution.py:12
  128.0 5.6 %collective-permute-start.5 = (f32[256,128]{0,1:T(8,128)S(1)}, f32[256,128]{0,1:T(8,128)S(1)}, u32[]{:S(2)}, u32[]{:S(2)}) collective-permute-start(f32[256,128]{0,1:T(8,128)S(1)} %get-tuple-element.12), channel_id=1, source_target_pairs={{1,0},{2,1},{3,2},{4,3},{5,4},{6,5},{7,6},{9,8},{10,9},{11,10},{12... | collective-permute-start | bytes 393224 | tf_op jit(solution)/shard_map/ppermute | solution.py:12
  131.1 2.5 %copy-start.4 = (f32[256,128]{0,1:T(8,128)}, f32[256,128]{0,1:T(8,128)S(1)}, u32[]{:S(2)}) copy-start(f32[256,128]{0,1:T(8,128)S(1)} %collective-permute-done.4) | copy-start | bytes 393220
  131.1 3.0 %copy-start.5 = (f32[256,128]{0,1:T(8,128)}, f32[256,128]{0,1:T(8,128)S(1)}, u32[]{:S(2)}) copy-start(f32[256,128]{0,1:T(8,128)S(1)} %collective-permute-done.7) | copy-start | bytes 393220
  131.1 3.0 %copy-start.6 = (f32[256,128]{0,1:T(8,128)}, f32[256,128]{0,1:T(8,128)S(1)}, u32[]{:S(2)}) copy-start(f32[256,128]{0,1:T(8,128)S(1)} %collective-permute-done.6) | copy-start | bytes 393220
  133.6 0.7 copy-start.7
  184.0 2.9 %copy-start.2 = (bf16[1,1,1024,1024]{3,2,1,0:T(8,128)(2,1)S(1)}, bf16[1,1,1024,1024]{3,2,1,0:T(8,128)(2,1)}, u32[]{:S(2)}) copy-start(bf16[1,1,1024,1024]{3,2,1,0:T(8,128)(2,1)} %param.9) | copy-start | bytes 6291460
  185.9 46.7 %copy-start.9 = (f32[1024]{0:T(1024)S(1)}, f32[1024]{0:T(1024)}, u32[]{:S(2)}) copy-start(f32[1024]{0:T(1024)} %copy-done.8) | copy-start | bytes 12292
  185.9 46.7 %copy-start.12 = (f32[1024]{0:T(1024)S(1)}, f32[1024]{0:T(1024)}, u32[]{:S(2)}) copy-start(f32[1024]{0:T(1024)} %copy-done.11) | copy-start | bytes 12292
  185.9 46.6 %copy-start.15 = (f32[128]{0:T(128)S(1)}, f32[128]{0:T(128)}, u32[]{:S(2)}) copy-start(f32[128]{0:T(128)} %copy-done.14) | copy-start | bytes 1540
where the time goes:
time: 236 us; the launch traced here: 235 us
  blocking collectives  187 us (79%)
  starting transfers between devices  21.7 us (9%)
  matrix products  15.4 us (7%)
  waiting for transfers between devices  4.82 us (2%)
  local copies, waits for them, and re-layouts  4.43 us (2%)
    psum x2, blocking collectives, local(): gain = lax.psum(gain_local, ('row', 'col'))  89.4 us
    psum x2, blocking collectives, local(): total = lax.psum(partial_value, 'col')  41.7 us
    psum x2, blocking collectives, broadcast(): return lax.psum(block, axis)  32.7 us
    all_gather x2, blocking collectives, local(): gathered = lax.all_gather(corner_force, 'row', axis=0, tiled=True)  22.8 us
    ppermute x8, starting transfers between devices, passed_along(): return lax.ppermute(x, axis, pairs)  21.7 us
    dot_general x2, matrix products, local(): jnp.dot(flex_block, lam.astype(jnp.bfloat16), preferred_element_type=jnp....  4.86 us
    ppermute x8, waiting for transfers between devices, passed_along(): return lax.ppermute(x, axis, pairs)  4.82 us
  transfers between devices with their start and end apart: 8, of which 3 were waited for; matrix products, arithmetic and copies ran while one was open for 0% of the time, Pallas kernels for 0%

commit v1 on v0

--- a/solution.py
+++ b/solution.py
@@ -68,7 +68,7 @@
         search = jnp.dot(schur_block, projected_b, preferred_element_type=jnp.float32)
         gain_local = jnp.sum(projected_b.astype(jnp.float32) * search, axis=0)
         search_b = search.astype(jnp.bfloat16)
-        gain = lax.psum(gain_local, ("row", "col"))
+        gain = lax.psum(lax.psum(gain_local, "col"), "row")
         curved = jnp.dot(flex_block, search_b, preferred_element_type=jnp.float32)
         curvature = lax.psum(jnp.sum(search_b.astype(jnp.float32) * curved, axis=0), ("row", "col"))
         lam = jnp.clip(lam - (gain / curvature)[None, :] * search, -bound, bound)

time: 236 us -> 282 us (1.19)
  blocking collectives: 187 us -> 229 us
  matrix products: 15.4 us -> 18.3 us
    psum x2 -> x6, blocking collectives: 89.4 us -> 130 us  [the longest x2 84.4 us: local(): lax.psum(jnp.sum(search_b.astype(jnp.float32) * curved, axis=0), ('row',...]
    dot_general x2, matrix products: 1.85 us -> 5 us  [local(): curved = jnp.dot(flex_block, search_b, preferred_element_type=jnp.float32)]
  transfers between devices with their start and end apart: 8 -> 8, of which waited for: 3 -> 4; matrix products, arithmetic and copies ran while one was open for 0% -> 0% of each run, Pallas kernels for 0% -> 0%
where the time goes in v1:
time: 282 us; the launch traced here: 280 us
  blocking collectives  229 us (81%)
  starting transfers between devices  21.7 us (8%)
  matrix products  18.3 us (6%)
  waiting for transfers between devices  4.83 us (2%)
  local copies, waits for them, and re-layouts  4.42 us (2%)
    psum x2, blocking collectives, local(): lax.psum(jnp.sum(search_b.astype(jnp.float32) * curved, axis=0), ('row',...  84.4 us
    psum x4, blocking collectives, local(): gain = lax.psum(lax.psum(gain_local, 'col'), 'row')  46.1 us
    psum x2, blocking collectives, local(): total = lax.psum(partial_value, 'col')  41.6 us
    psum x2, blocking collectives, broadcast(): return lax.psum(block, axis)  34 us
    all_gather x2, blocking collectives, local(): gathered = lax.all_gather(corner_force, 'row', axis=0, tiled=True)  22.8 us
    ppermute x8, starting transfers between devices, passed_along(): return lax.ppermute(x, axis, pairs)  21.7 us
  transfers between devices with their start and end apart: 8, of which 4 were waited for; matrix products, arithmetic and copies ran while one was open for 0% of the time, Pallas kernels for 0%

profile of v1, /device:TPU:14, one launch (start us, length us, event | category | flops | bytes accessed | tf_op | source)
XLA Modules:
  0.0 280.4 jit_solution(7773075990904049246)
XLA Ops:
  1.0 1.1 copy.15
  2.1 2.4 fusion.14
  5.3 1.9 collective-permute-start
  7.2 2.4 collective-permute-start.3
  9.6 3.5 %collective-permute-start.2 = (f32[256,128]{0,1:T(8,128)}, f32[256,128]{0,1:T(8,128)S(1)}, u32[]{:S(2)}, u32[]{:S(2)}) collective-permute-start(f32[256,128]{0,1:T(8,128)} %get-tuple-element.11), channel_id=1, source_target_pairs={{0,8},{8,16},{16,24},{1,9},{9,17},{17,25},{2,10},{10,18},{18,26},{... | collective-permute-start | bytes 393224 | tf_op jit(solution)/shard_map/ppermute | solution.py:12
  13.1 3.1 %collective-permute-start.1 = (f32[256,128]{0,1:T(8,128)S(1)}, f32[256,128]{0,1:T(8,128)}, u32[]{:S(2)}, u32[]{:S(2)}) collective-permute-start(f32[256,128]{0,1:T(8,128)S(1)} %get-tuple-element.12), channel_id=1, source_target_pairs={{1,0},{2,1},{3,2},{4,3},{5,4},{6,5},{7,6},{9,8},{10,9},{11,10},{12... | collective-permute-start | bytes 393224 | tf_op jit(solution)/shard_map/ppermute | solution.py:12
  16.6 2.0 collective-permute-done.1
  18.7 1.5 convolution_bitcast_fusion.5
  20.1 11.5 %all-gather = f32[4,12,128]{2,1,0:T(8,128)S(1)} all-gather(f32[1,12,128]{2,1,0:T(8,128)S(1)} %convolution_bitcast_fusion.5), channel_id=1, replica_groups=mesh['row'=4,'col'=8] {'row'}, dimensions={0}, use_global_device_ids=true | all-gather | bytes 30720 | tf_op jit(solution)/shard_map/all_gather | solution.py:57
  31.9 21.2 %psum.70 = f32[96,128]{1,0:T(8,128)S(1)} all-reduce(f32[96,128]{1,0:T(8,128)S(1)} %convolution_bitcast_fusion.3), channel_id=1, replica_groups=mesh['row'=4,'col'=8] {'col'}, use_global_device_ids=true, to_apply=%region_1.2 | all-reduce | flops 12288 | bytes 98304 | tf_op jit(solution)/shard_map/psum | solution.py:59
  53.1 16.4 %psum.71 = f32[96,128]{1,0:T(8,128)S(1)} all-reduce(f32[96,128]{1,0:T(8,128)S(1)} %broadcast_select_fusion.1), channel_id=1, replica_groups=mesh['row'=4,'col'=8] {'row'}, use_global_device_ids=true, to_apply=%region_2.3 | all-reduce | flops 12288 | bytes 98304 | tf_op jit(solution)/shard_map/psum | solution.py:17
  69.5 1.5 fusion.39
  71.9 11.9 %psum.72 = f32[128]{0:T(128)S(1)} all-reduce(f32[128]{0:T(128)S(1)} %get-tuple-element.13), channel_id=1, replica_groups=mesh['row'=4,'col'=8] {'col'}, use_global_device_ids=true, to_apply=%region_4.5 | all-reduce | flops 128 | bytes 1024 | tf_op jit(solution)/shard_map/psum | solution.py:71
  83.9 11.7 %psum.73 = f32[128]{0:T(128)S(1)} all-reduce(f32[128]{0:T(128)S(1)} %psum.72), channel_id=1, replica_groups=mesh['row'=4,'col'=8] {'row'}, use_global_device_ids=true, to_apply=%region_5.6 | all-reduce | flops 128 | bytes 1024 | tf_op jit(solution)/shard_map/psum | solution.py:71
  95.5 2.5 fusion.40
  98.0 41.7 %psum.74 = f32[128]{0:T(128)S(1)} all-reduce(f32[128]{0:T(128)S(1)} %fusion.40), channel_id=1, replica_groups=mesh['row'=4,'col'=8] {'row','col'}, use_global_device_ids=true, to_apply=%region_7.8 | all-reduce | flops 128 | bytes 1024 | tf_op jit(solution)/shard_map/psum | solution.py:73
  139.7 2.4 fusion.20
  142.2 1.9 collective-permute-start.4
  144.1 3.4 %collective-permute-start.7 = (f32[256,128]{0,1:T(8,128)S(1)}, f32[256,128]{0,1:T(8,128)S(1)}, u32[]{:S(2)}, u32[]{:S(2)}) collective-permute-start(f32[256,128]{0,1:T(8,128)S(1)} %get-tuple-element.6), channel_id=1, source_target_pairs={{8,0},{16,8},{24,16},{9,1},{17,9},{25,17},{10,2},{18,10},{26,18},{... | collective-permute-start | bytes 393224 | tf_op jit(solution)/shard_map/ppermute | solution.py:12
  147.5 2.5 collective-permute-start.6
  150.0 3.1 %collective-permute-start.5 = (f32[256,128]{0,1:T(8,128)S(1)}, f32[256,128]{0,1:T(8,128)S(1)}, u32[]{:S(2)}, u32[]{:S(2)}) collective-permute-start(f32[256,128]{0,1:T(8,128)S(1)} %get-tuple-element.8), channel_id=1, source_target_pairs={{1,0},{2,1},{3,2},{4,3},{5,4},{6,5},{7,6},{9,8},{10,9},{11,10},{12... | collective-permute-start | bytes 393224 | tf_op jit(solution)/shard_map/ppermute | solution.py:12
  153.1 1.3 collective-permute-done.6
  154.4 1.2 collective-permute-done.5
  156.3 11.4 %all-gather.1 = f32[4,12,128]{2,1,0:T(8,128)S(1)} all-gather(f32[1,12,128]{2,1,0:T(8,128)S(1)} %convolution_bitcast_fusion.4), channel_id=1, replica_groups=mesh['row'=4,'col'=8] {'row'}, dimensions={0}, use_global_device_ids=true | all-gather | bytes 30720 | tf_op jit(solution)/shard_map/all_gather | solution.py:57
  169.2 20.4 %psum.75 = f32[96,128]{1,0:T(8,128)S(1)} all-reduce(f32[96,128]{1,0:T(8,128)S(1)} %convolution_bitcast_fusion.2), channel_id=1, replica_groups=mesh['row'=4,'col'=8] {'col'}, use_global_device_ids=true, to_apply=%region_8.9 | all-reduce | flops 12288 | bytes 98304 | tf_op jit(solution)/shard_map/psum | solution.py:59
  189.7 17.6 %psum.76 = f32[96,128]{1,0:T(8,128)S(1)} all-reduce(f32[96,128]{1,0:T(8,128)S(1)} %broadcast_select_fusion), channel_id=1, replica_groups=mesh['row'=4,'col'=8] {'row'}, use_global_device_ids=true, to_apply=%region_9.10 | all-reduce | flops 12288 | bytes 98304 | tf_op jit(solution)/shard_map/psum | solution.py:17
  207.2 1.8 fusion.38
  209.9 11.8 %psum.77 = f32[128]{0:T(128)S(1)} all-reduce(f32[128]{0:T(128)S(1)} %get-tuple-element.15), channel_id=1, replica_groups=mesh['row'=4,'col'=8] {'col'}, use_global_device_ids=true, to_apply=%region_11.12 | all-reduce | flops 128 | bytes 1024 | tf_op jit(solution)/shard_map/psum | solution.py:71
  221.8 10.7 %psum.78 = f32[128]{0:T(128)S(1)} all-reduce(f32[128]{0:T(128)S(1)} %psum.77), channel_id=1, replica_groups=mesh['row'=4,'col'=8] {'row'}, use_global_device_ids=true, to_apply=%region_12.13 | all-reduce | flops 128 | bytes 1024 | tf_op jit(solution)/shard_map/psum | solution.py:71
  232.4 2.5 fusion.43
  234.9 42.7 %psum.79 = f32[128]{0:T(128)S(1)} all-reduce(f32[128]{0:T(128)S(1)} %fusion.43), channel_id=1, replica_groups=mesh['row'=4,'col'=8] {'row','col'}, use_global_device_ids=true, to_apply=%region_14.15 | all-reduce | flops 128 | bytes 1024 | tf_op jit(solution)/shard_map/psum | solution.py:73
  278.6 1.8 copy.16
  (53 shorter events, 7.6 us)
Async XLA Ops:
  0.0 71.0 %copy-start = (bf16[1,1,1024,1024]{3,2,1,0:T(8,128)(2,1)S(1)}, bf16[1,1,1024,1024]{3,2,1,0:T(8,128)(2,1)}, u32[]{:S(2)}) copy-start(bf16[1,1,1024,1024]{3,2,1,0:T(8,128)(2,1)} %param.10) | copy-start | bytes 6291460
  0.9 138.8 %copy-start.6 = (f32[1024]{0:T(1024)}, f32[1024]{0:T(1024)S(1)}, u32[]{:S(2)}) copy-start(f32[1024]{0:T(1024)S(1)} %select_reduce_fusion) | copy-start | bytes 12292
  1.0 138.8 %copy-start.9 = (f32[1024]{0:T(1024)}, f32[1024]{0:T(1024)S(1)}, u32[]{:S(2)}) copy-start(f32[1024]{0:T(1024)S(1)} %neg.10) | copy-start | bytes 12292
  2.1 14.1 %copy-start.14 = (s32[1,1,4]{2,1,0:T(1,128)S(1)}, s32[1,1,4]{2,1,0:T(1,128)}, u32[]{:S(2)}) copy-start(s32[1,1,4]{2,1,0:T(1,128)} %param.15) | copy-start | bytes 52
  2.1 16.6 %copy-start.1 = (f32[1,1,12,1024]{3,1,2,0:T(1,128)S(1)}, f32[1,1,12,1024]{3,1,2,0:T(1,128)}, u32[]{:S(2)}) copy-start(f32[1,1,12,1024]{3,1,2,0:T(1,128)} %param.11) | copy-start | bytes 147460
  2.1 29.5 %copy-start.8 = (f32[96,48]{0,1:T(8,128)S(1)}, f32[96,48]{0,1:T(8,128)}, u32[]{:S(2)}) copy-start(f32[96,48]{0,1:T(8,128)} %param.12) | copy-start | bytes 55300
  5.3 11.0 %collective-permute-start = (f32[256,128]{0,1:T(8,128)}, f32[256,128]{0,1:T(8,128)S(1)}, u32[]{:S(2)}, u32[]{:S(2)}) collective-permute-start(f32[256,128]{0,1:T(8,128)} %get-tuple-element.9), channel_id=1, source_target_pairs={{0,1},{1,2},{2,3},{3,4},{4,5},{5,6},{6,7},{8,9},{9,10},{10,11},{11... | collective-permute-start | bytes 393224 | tf_op jit(solution)/shard_map/ppermute | solution.py:12
  7.2 9.1 %collective-permute-start.3 = (f32[256,128]{0,1:T(8,128)}, f32[256,128]{0,1:T(8,128)S(1)}, u32[]{:S(2)}, u32[]{:S(2)}) collective-permute-start(f32[256,128]{0,1:T(8,128)} %get-tuple-element.10), channel_id=1, source_target_pairs={{8,0},{16,8},{24,16},{9,1},{17,9},{25,17},{10,2},{18,10},{26,18},{... | collective-permute-start | bytes 393224 | tf_op jit(solution)/shard_map/ppermute | solution.py:12
  9.6 7.1 %collective-permute-start.2 = (f32[256,128]{0,1:T(8,128)}, f32[256,128]{0,1:T(8,128)S(1)}, u32[]{:S(2)}, u32[]{:S(2)}) collective-permute-start(f32[256,128]{0,1:T(8,128)} %get-tuple-element.11), channel_id=1, source_target_pairs={{0,8},{8,16},{16,24},{1,9},{9,17},{17,25},{2,10},{10,18},{18,26},{... | collective-permute-start | bytes 393224 | tf_op jit(solution)/shard_map/ppermute | solution.py:12
  13.1 5.6 %collective-permute-start.1 = (f32[256,128]{0,1:T(8,128)S(1)}, f32[256,128]{0,1:T(8,128)}, u32[]{:S(2)}, u32[]{:S(2)}) collective-permute-start(f32[256,128]{0,1:T(8,128)S(1)} %get-tuple-element.12), channel_id=1, source_target_pairs={{1,0},{2,1},{3,2},{4,3},{5,4},{6,5},{7,6},{9,8},{10,9},{11,10},{12... | collective-permute-start | bytes 393224 | tf_op jit(solution)/shard_map/ppermute | solution.py:12
  16.3 139.3 %copy-start.11 = (f32[1,2,4,128]{3,1,2,0:T(2,128)}, f32[1,2,4,128]{3,1,2,0:T(2,128)S(1)}, u32[]{:S(2)}) copy-start(f32[1,2,4,128]{3,1,2,0:T(2,128)S(1)} %copy.18) | copy-start | bytes 12292
  139.7 2.5 copy-start.12
  142.2 10.9 %collective-permute-start.4 = (f32[256,128]{0,1:T(8,128)S(1)}, f32[256,128]{0,1:T(8,128)S(1)}, u32[]{:S(2)}, u32[]{:S(2)}) collective-permute-start(f32[256,128]{0,1:T(8,128)S(1)} %get-tuple-element.5), channel_id=1, source_target_pairs={{0,1},{1,2},{2,3},{3,4},{4,5},{5,6},{6,7},{8,9},{9,10},{10,11},{11... | collective-permute-start | bytes 393224 | tf_op jit(solution)/shard_map/ppermute | solution.py:12
  144.1 9.0 %collective-permute-start.7 = (f32[256,128]{0,1:T(8,128)S(1)}, f32[256,128]{0,1:T(8,128)S(1)}, u32[]{:S(2)}, u32[]{:S(2)}) collective-permute-start(f32[256,128]{0,1:T(8,128)S(1)} %get-tuple-element.6), channel_id=1, source_target_pairs={{8,0},{16,8},{24,16},{9,1},{17,9},{25,17},{10,2},{18,10},{26,18},{... | collective-permute-start | bytes 393224 | tf_op jit(solution)/shard_map/ppermute | solution.py:12
  147.5 6.9 %collective-permute-start.6 = (f32[256,128]{0,1:T(8,128)S(1)}, f32[256,128]{0,1:T(8,128)S(1)}, u32[]{:S(2)}, u32[]{:S(2)}) collective-permute-start(f32[256,128]{0,1:T(8,128)S(1)} %get-tuple-element.7), channel_id=1, source_target_pairs={{0,8},{8,16},{16,24},{1,9},{9,17},{17,25},{2,10},{10,18},{18,26},{... | collective-permute-start | bytes 393224 | tf_op jit(solution)/shard_map/ppermute | solution.py:12
  150.0 5.6 %collective-permute-start.5 = (f32[256,128]{0,1:T(8,128)S(1)}, f32[256,128]{0,1:T(8,128)S(1)}, u32[]{:S(2)}, u32[]{:S(2)}) collective-permute-start(f32[256,128]{0,1:T(8,128)S(1)} %get-tuple-element.8), channel_id=1, source_target_pairs={{1,0},{2,1},{3,2},{4,3},{5,4},{6,5},{7,6},{9,8},{10,9},{11,10},{12... | collective-permute-start | bytes 393224 | tf_op jit(solution)/shard_map/ppermute | solution.py:12
  153.1 2.5 copy-start.2
  153.1 3.0 %copy-start.3 = (f32[256,128]{0,1:T(8,128)}, f32[256,128]{0,1:T(8,128)S(1)}, u32[]{:S(2)}) copy-start(f32[256,128]{0,1:T(8,128)S(1)} %collective-permute-done.7) | copy-start | bytes 393220
  154.4 1.8 copy-start.4
  155.6 0.7 copy-start.5
  209.0 68.6 %copy-start.7 = (f32[1024]{0:T(1024)S(1)}, f32[1024]{0:T(1024)}, u32[]{:S(2)}) copy-start(f32[1024]{0:T(1024)} %copy-done.6) | copy-start | bytes 12292
  209.0 68.6 %copy-start.10 = (f32[1024]{0:T(1024)S(1)}, f32[1024]{0:T(1024)}, u32[]{:S(2)}) copy-start(f32[1024]{0:T(1024)} %copy-done.9) | copy-start | bytes 12292
  209.0 68.6 %copy-start.13 = (f32[128]{0:T(128)S(1)}, f32[128]{0:T(128)}, u32[]{:S(2)}) copy-start(f32[128]{0:T(128)} %copy-done.12) | copy-start | bytes 1540
